TPU v7x, 256 devices: a whole 4x4x8 slice. The times are simulated.
256 devices in a mesh: ctx: 16 (over y_hi, z), head: 8 (over x, core), rep: 2 (over y_lo).
Axes of the slice: x: 4, y: 4 (y_hi: 2, y_lo: 2; y = y_hi * 2 + y_lo), z: 8, core: 2. Of those that a mesh axis runs over, the one named last changes fastest.
Arguments:
- query_latent: bfloat16 [8192, 1536], P(('rep', 'ctx')), parts along dimension 0, may hold values from -6 to 6
- key_rows: bfloat16 [8192, 576], P(('rep', 'ctx')), parts along dimension 0, may hold values from -640 to 640
- key_cache: bfloat16 [1024, 576], P('rep'), parts along dimension 0, may hold values from -640 to 640
- prompt_start: int32 [2], P('rep'), parts along dimension 0, may hold values from 0 to 512
- w_query: bfloat16 [1536, 12288], P(None, 'head'), may hold values from -0.15625 to 0.15625
- w_key_up: bfloat16 [64, 128, 512], P('head'), may hold values from -0.5 to 0.5
- w_value_up: bfloat16 [64, 512, 128], P('head'), may hold values from -0.25 to 0.25
- w_output: bfloat16 [64, 128, 7168], P('head', 'ctx'), may hold values from -0.09375 to 0.09375
Outputs:
- layer_out: bfloat16 [8192, 7168], P(('rep', 'ctx'), 'head'), parts along dimension 0
There are 2 independent parts, one for each index of `rep`. A program takes and returns all parts, laid end to end along the dimension named above; an argument that names none is the same for every part. Nothing has to cross between parts.
All inputs are finite; a program needn't handle non-finite values.
Results may differ from a plain program's by a relative error of at most 0.017.
The roundings to bfloat16 on the way count: a program that leaves them out, or rounds other values in their place, can miss the bound.
Values may be sent and summed in bfloat16 or wider, within the bound.
No kernel may reach another device: no remote copies, remote signals or barrier semaphores. Data moves between devices by JAX's collectives and lax.ppermute only.
A program may use at most 128 MiB of HBM per device.

v0:
```python
import jax
import jax.numpy as jnp
from jax import lax
from jax.sharding import PartitionSpec as P


def passed_along(x, axis, by):
    devices = lax.axis_size(axis)
    pairs = [(i, i + by) for i in range(devices) if 0 <= i + by < devices]
    return lax.ppermute(x, axis, pairs)


def rotate(values, positions):
    half_dim = values.shape[-1] // 2
    inverse = jnp.power(
        jnp.float32(10000.0), -jnp.arange(half_dim, dtype=jnp.float32) * (2.0 / values.shape[-1])
    )
    angles = positions[..., None] * inverse
    cosine = jnp.cos(angles)
    sines = jnp.sin(angles)
    lower_half = values[..., :half_dim]
    upper_half = values[..., half_dim:]
    return jnp.concatenate(
        [lower_half * cosine - upper_half * sines, lower_half * sines + upper_half * cosine], -1
    )


def local(query_latent, key_rows, key_cache, prompt_start, w_query, w_key_up, w_value_up, w_output):
    tok_rows = query_latent.shape[0]
    heads_dev, nope_dim, latent = w_key_up.shape
    rope_dim = key_rows.shape[1] - latent
    window = key_cache.shape[0]
    slab_index = lax.axis_index("ctx")
    queries = jnp.dot(query_latent, w_query, preferred_element_type=jnp.float32).astype(
        jnp.bfloat16
    )
    queries = queries.reshape(tok_rows, heads_dev, nope_dim + rope_dim)
    query_lat = jnp.einsum(
        "thn,hnl->thl", queries[..., :nope_dim], w_key_up, preferred_element_type=jnp.float32
    ).astype(jnp.bfloat16)
    token_pos = (slab_index * tok_rows + jnp.arange(tok_rows, dtype=jnp.int32)).astype(jnp.float32)
    query_rot = rotate(queries[..., nope_dim:].astype(jnp.float32), token_pos[:, None]).astype(
        jnp.bfloat16
    )
    key_rot = rotate(key_rows[:, latent:].astype(jnp.float32), token_pos).astype(jnp.bfloat16)
    own_keys = jnp.concatenate([key_rows[:, :latent], key_rot], 1)
    piece_rows = min(tok_rows, window)
    hop_count = window // piece_rows
    received = []
    for hop_number in range(hop_count):
        received.append(passed_along(own_keys, "ctx", hop_number + 1))
    key_blocks = []
    for hop_number in range(hop_count):
        distance = hop_number + 1
        cache_slot = jnp.clip(hop_count - distance + slab_index, 0, hop_count - 1)
        cached = lax.dynamic_slice_in_dim(key_cache, cache_slot * piece_rows, piece_rows, 0)
        key_blocks.append(jnp.where(slab_index < distance, cached, received[hop_number]))
    all_keys = jnp.concatenate(key_blocks[::-1] + [own_keys], 0)
    key_span = all_keys.shape[0]
    key_lat = all_keys[:, :latent]
    score_scale = (nope_dim + rope_dim) ** (-0.5)
    scores = jnp.einsum("thl,kl->htk", query_lat, key_lat, preferred_element_type=jnp.float32)
    scores = scores + jnp.einsum(
        "thr,kr->htk", query_rot, all_keys[:, latent:], preferred_element_type=jnp.float32
    )
    scores = scores * score_scale
    key_pos = jnp.arange(key_span, dtype=jnp.int32) - window
    row_ids = jnp.arange(tok_rows, dtype=jnp.int32)
    relative = key_pos[None, :] - row_ids[:, None]
    in_prompt = slab_index * tok_rows + key_pos >= -prompt_start[0]
    visible = (relative <= 0) & (relative > -window) & in_prompt[None, :]
    scores = jnp.where(visible[None], scores, -1e30)
    row_max = jnp.max(scores, axis=-1, keepdims=True)
    powers = jnp.exp(scores - row_max)
    weights = (powers / jnp.sum(powers, axis=-1, keepdims=True)).astype(jnp.bfloat16)
    mixed_lat = jnp.einsum(
        "htk,kl->thl", weights, key_lat, preferred_element_type=jnp.float32
    ).astype(jnp.bfloat16)
    attention = jnp.einsum(
        "thl,hlv->thv", mixed_lat, w_value_up, preferred_element_type=jnp.float32
    ).astype(jnp.bfloat16)
    full_rows = lax.all_gather(w_output, "ctx", axis=1, tiled=True)
    flat_attention = attention.reshape(tok_rows, -1)
    flat_rows = full_rows.reshape(-1, full_rows.shape[2])
    partial_value = jnp.dot(flat_attention, flat_rows, preferred_element_type=jnp.float32)
    return lax.psum_scatter(partial_value, "head", scatter_dimension=1, tiled=True).astype(
        jnp.bfloat16
    )


def solution(mesh):
    return jax.shard_map(
        local,
        mesh=mesh,
        in_specs=(
            P(("rep", "ctx"), None),
            P(("rep", "ctx"), None),
            P("rep", None),
            P("rep"),
            P(None, "head"),
            P("head", None, None),
            P("head", None, None),
            P("head", "ctx", None),
        ),
        out_specs=P(("rep", "ctx"), "head"),
        check_vma=False,
    )
```

profile of v0, /device:TPU:1, one launch (start us, length us, event | category | flops | bytes accessed | tf_op | source)
XLA Modules:
  0.0 288.0 jit_solution(6459296274716134943)
XLA Ops:
  6.5 0.0 copy-start
  6.5 0.0 all-gather.2.cloned.1.call-start
  6.5 0.7 all-gather.2.cloned.1.call-update
  7.3 0.0 reduce-scatter.2.cloned.1.call-start
  7.3 1.0 slice.30
  8.3 0.8 slice_convert_fusion.1
  9.1 0.2 multiply_cosine_fusion
  9.3 0.1 copy.27
  9.4 0.1 copy.28
  9.5 0.1 copy.43
  9.7 0.8 pad_maximum_fusion
  10.5 6.4 %collective-permute-start = (bf16[256,576]{1,0:T(8,128)(2,1)}, bf16[256,576]{1,0:T(8,128)(2,1)}, u32[]{:S(2)}, u32[]{:S(2)}) collective-permute-start(bf16[256,576]{1,0:T(8,128)(2,1)} %pad_maximum_fusion), channel_id=1, source_target_pairs={{0,32},{16,48},{32,64},{48,80},{64,96},{80,112},{96,128},{112,144}... | collective-permute-start | bytes 884744 | tf_op jit(solution)/shard_map/ppermute | solution.py:10
  16.9 4.3 %collective-permute-start.1 = (bf16[256,576]{1,0:T(8,128)(2,1)}, bf16[256,576]{1,0:T(8,128)(2,1)}, u32[]{:S(2)}, u32[]{:S(2)}) collective-permute-start(bf16[256,576]{1,0:T(8,128)(2,1)} %pad_maximum_fusion), channel_id=1, source_target_pairs={{0,16},{16,32},{32,48},{48,64},{64,80},{80,96},{96,112},{112,128},... | collective-permute-start | bytes 884744 | tf_op jit(solution)/shard_map/ppermute | solution.py:10
  21.2 4.0 %convolution_convert_fusion = bf16[256,1536]{1,0:T(8,128)(2,1)S(1)} fusion(bf16[256,1536]{1,0:T(8,128)(2,1)} %param.8, bf16[1536,1536]{1,0:T(8,128)(2,1)} %param.12), kind=kOutput, calls=%fused_computation.6 | convolution fusion | flops 1208352768 | bytes 6291456 | tf_op jit(solution)/shard_map/dot_general | solution.py:34
  25.2 0.3 copy.30
  26.2 0.7 subtract_convert_fusion
  26.9 0.3 fusion.18
  27.2 1.1 constant_dynamic-slice_fusion.1
  28.4 0.2 copy.42
  28.6 0.2 copy.44
  28.8 0.0 collective-permute-done
  28.8 0.1 broadcast_select_fusion.1
  28.8 11.8 %collective-permute-done.1 = bf16[256,576]{1,0:T(8,128)(2,1)} collective-permute-done((bf16[256,576]{1,0:T(8,128)(2,1)}, bf16[256,576]{1,0:T(8,128)(2,1)}, u32[]{:S(2)}, u32[]{:S(2)}) %collective-permute-start.1) | collective-permute-done | bytes 294944 | tf_op jit(solution)/shard_map/ppermute | solution.py:10
  40.7 0.0 copy-start.3
  40.7 1.1 maximum_maximum_fusion
  41.8 0.0 copy-done
  41.8 6.1 %fusion.2 = f32[768,256,8]{1,0,2:T(8,128)} fusion(bf16[8,128,512]{2,1,0:T(8,128)(2,1)S(1)} %copy-done, bf16[768,576]{1,0:T(8,128)(2,1)} %maximum_maximum_fusion, bf16[256,8,192]{0,2,1:T(8,128)(2,1)S(1)} %bitcast.29), kind=kOutput, calls=%fused_computation.7 | convolution fusion | flops 1880096768 | bytes 8650752 | tf_op jit(solution)/shard_map/thl,kl->htk/dot_general | solution.py:62
  47.9 0.0 copy-done.3
  47.9 4.0 %bitcast_select_fusion = f32[8,256,768]{1,2,0:T(8,128)S(1)} fusion(f32[768,256,8]{1,0,2:T(8,128)} %fusion.2, pred[256,768]{0,1:T(8,128)(4,1)S(1)} %fusion.18, bf16[256,8,32]{0,2,1:T(8,128)(2,1)S(1)} %copy-done.3, bf16[256,8,32]{0,2,1:T(8,128)(2,1)S(1)} %get-tuple-element.5, bf16[256,32]{1,0:T(8,128)(2,1)S(1)} %copy.28, ...), kind=kOutput, calls=%fused_computation.2 | convolution fusion | flops 207060992 | bytes 13926400 | tf_op jit(solution)/shard_map/thr,kr->htk/dot_general | solution.py:63
  52.0 0.0 copy-start.1
  52.0 2.6 copy-done.1
  54.5 0.0 copy-start.2
  54.5 1.1 fusion.35
  55.7 0.1 copy-done.2
  55.8 7.8 %fusion.12 = bf16[256,8,128]{2,0,1:T(8,128)(2,1)S(1)} fusion(bf16[8,512,128]{2,1,0:T(8,128)(2,1)} %param.14, f32[8,256]{1,0:T(8,128)S(1)} %fusion.35, bf16[768,576]{1,0:T(8,128)(2,1)S(1)} %copy-done.2, f32[8,256,768]{1,2,0:T(8,128)} %copy-done.1), kind=kOutput, calls=%fused_computation.14 | convolution fusion | flops 1885080320 | bytes 14950400 | tf_op jit(solution)/shard_map/thl,hlv->thv/dot_general | solution.py:79
  63.5 159.8 %all-gather.2.cloned.1.call-done = bf16[8,128,7168]{2,1,0:T(8,128)(2,1)} async-done(((bf16[8,8,7168]{2,1,0:T(8,128)(2,1)}), bf16[8,128,7168]{2,1,0:T(8,128)(2,1)}) %all-gather.2.cloned.1.call-update) | async-done | bytes 14680080 | tf_op jit(solution)/shard_map/all_gather | solution.py:82
  223.3 9.1 %convolution_bitcast_fusion = f32[256,7168]{1,0:T(8,128)} fusion(bf16[256,8,128]{2,0,1:T(8,128)(2,1)S(1)} %fusion.12, bf16[8,128,7168]{2,1,0:T(8,128)(2,1)} %all-gather.2.cloned.1.call-done), kind=kOutput, calls=%fused_computation.1 | convolution fusion | flops 3758096384 | bytes 22544384 | tf_op jit(solution)/shard_map/dot_general | solution.py:85
  232.4 0.0 reduce-scatter.2.cloned.1.call-update
  232.4 46.8 %reduce-scatter.2.cloned.1.call-done = f32[256,896]{1,0:T(8,128)} async-done(((f32[256,7168]{1,0:T(8,128)}), f32[256,896]{1,0:T(8,128)}) %reduce-scatter.2.cloned.1.call-update) | async-done | bytes 917520 | tf_op jit(solution)/shard_map/reduce_scatter | solution.py:86
  279.2 2.0 convert_element_type.54
  (6 shorter events, 0.1 us)
Async XLA Ops:
  6.5 35.3 %copy-start = (bf16[8,128,512]{2,1,0:T(8,128)(2,1)S(1)}, bf16[8,128,512]{2,1,0:T(8,128)(2,1)}, u32[]{:S(2)}) copy-start(bf16[8,128,512]{2,1,0:T(8,128)(2,1)} %param.13) | copy-start | bytes 3145732
  6.5 216.8 %all-gather.2.cloned.1.call-start = ((), (), s32[]{:S(2)}) async-start(), calls=%async_computation.1 | async-start | bytes 15597568 | tf_op jit(solution)/shard_map/all_gather | solution.py:82
  7.3 271.9 %reduce-scatter.2.cloned.1.call-start = ((), (), s32[]{:S(2)}) async-start(), calls=%async_computation.2 | async-start | bytes 8257536 | tf_op jit(solution)/shard_map/reduce_scatter | solution.py:86
  10.5 18.3 %collective-permute-start = (bf16[256,576]{1,0:T(8,128)(2,1)}, bf16[256,576]{1,0:T(8,128)(2,1)}, u32[]{:S(2)}, u32[]{:S(2)}) collective-permute-start(bf16[256,576]{1,0:T(8,128)(2,1)} %pad_maximum_fusion), channel_id=1, source_target_pairs={{0,32},{16,48},{32,64},{48,80},{64,96},{80,112},{96,128},{112,144}... | collective-permute-start | bytes 884744 | tf_op jit(solution)/shard_map/ppermute | solution.py:10
  16.9 23.7 %collective-permute-start.1 = (bf16[256,576]{1,0:T(8,128)(2,1)}, bf16[256,576]{1,0:T(8,128)(2,1)}, u32[]{:S(2)}, u32[]{:S(2)}) collective-permute-start(bf16[256,576]{1,0:T(8,128)(2,1)} %pad_maximum_fusion), channel_id=1, source_target_pairs={{0,16},{16,32},{32,48},{48,64},{64,80},{80,96},{96,112},{112,128},... | collective-permute-start | bytes 884744 | tf_op jit(solution)/shard_map/ppermute | solution.py:10
  40.7 7.2 %copy-start.3 = (bf16[256,8,32]{0,2,1:T(8,128)(2,1)S(1)}, bf16[256,8,32]{0,2,1:T(8,128)(2,1)}, u32[]{:S(2)}) copy-start(bf16[256,8,32]{0,2,1:T(8,128)(2,1)} %get-tuple-element.6) | copy-start | bytes 393220
  52.0 2.6 copy-start.1
  54.5 1.2 copy-start.2
Sparse Core Ops, SparseCore 0:
  10.0 213.2 all-gather.1
  232.5 46.6 reduce-scatter.1
where the time goes:
time: 289 us; the launch traced here: 288 us
  waiting for transfers between devices  219 us (76%)
  matrix products  30.9 us (11%)
  between operations  14.2 us (5%)
  starting transfers between devices  10.8 us (4%)
  other arithmetic  7.18 us (2%)
  local copies, waits for them, and re-layouts  5.8 us (2%)
    all_gather x1, waiting for transfers between devices, local(): full_rows = lax.all_gather(w_output, 'ctx', axis=1, tiled=True)  160 us
    reduce_scatter x1, waiting for transfers between devices, local(): lax.psum_scatter(partial_value, 'head', scatter_dimension=1, tiled=True)  46.8 us
    ppermute x2, waiting for transfers between devices, passed_along(): return lax.ppermute(x, axis, pairs)  11.8 us
    ppermute x2, starting transfers between devices, passed_along(): return lax.ppermute(x, axis, pairs)  10.7 us
    dot_general x1, matrix products, local(): jnp.dot(flat_attention, flat_rows, preferred_element_type=jnp.float32)  9.08 us
    dot_general x1, matrix products, local(): jnp.einsum('thl,hlv->thv', mixed_lat, w_value_up, preferred_element_type=...  7.75 us
    dot_general x1, matrix products, local(): jnp.einsum('thl,kl->htk', query_lat, key_lat, preferred_element_type=jnp....  6.09 us
  transfers between devices with their start and end apart: 4, of which 3 were waited for; matrix products, arithmetic and copies ran while one was open for 10% of the time, Pallas kernels for 0%

commit v1 on v0

--- a/solution.py
+++ b/solution.py
@@ -79,7 +79,12 @@
     attention = jnp.einsum(
         "thl,hlv->thv", mixed_lat, w_value_up, preferred_element_type=jnp.float32
     ).astype(jnp.bfloat16)
-    full_rows = lax.all_gather(w_output, "ctx", axis=1, tiled=True)
+    full_rows = jnp.concatenate(
+        lax.all_to_all(
+            jnp.stack([w_output for _ in range(lax.psum(1, "ctx"))], axis=0), "ctx", 0, 0
+        ),
+        axis=1,
+    )
     flat_attention = attention.reshape(tok_rows, -1)
     flat_rows = full_rows.reshape(-1, full_rows.shape[2])
     partial_value = jnp.dot(flat_attention, flat_rows, preferred_element_type=jnp.float32)

time: 289 us -> 487 us (1.69)
  waiting for transfers between devices: 219 us -> 395 us
  local copies, waits for them, and re-layouts: 5.8 us -> 22.2 us
  starting transfers between devices: 10.8 us -> 19.9 us
    ppermute x2, waiting for transfers between devices: 11.8 us -> 329 us  [passed_along(): return lax.ppermute(x, axis, pairs)]
    all_gather x1 -> x0, waiting for transfers between devices: 160 us -> none  [local(): full_rows = lax.all_gather(w_output, 'ctx', axis=1, tiled=True)]
    reduce_scatter x1, waiting for transfers between devices: 46.8 us -> 66.1 us  [local(): lax.psum_scatter(partial_value, 'head', scatter_dimension=1, tiled=True)]
    all_to_all x0 -> x1, starting transfers between devices: none -> 11.9 us  [local(): lax.all_to_all(jnp.stack([w_output for _ in range(lax.psum(1, 'ctx'))], a...]
    another operation x2 -> x3, local copies, waits for them, and re-layouts: 0.24 us -> 8.56 us  [the longest x1 8.32 us: local(): jnp.stack([w_output for _ in range(lax.psum(1, 'ctx'))], axis=0)]
    all_to_all x0 -> x1, local copies, waits for them, and re-layouts: none -> 7.58 us  [local(): lax.all_to_all(jnp.stack([w_output for _ in range(lax.psum(1, 'ctx'))], a...]
  transfers between devices with their start and end apart: 4 -> 4, of which waited for: 3 -> 2; matrix products, arithmetic and copies ran while one was open for 10% -> 6% of each run, Pallas kernels for 0% -> 0%
where the time goes in v1:
time: 487 us
  waiting for transfers between devices  395 us (81%)
  matrix products  28.5 us (6%)
  local copies, waits for them, and re-layouts  22.2 us (5%)
  starting transfers between devices  19.9 us (4%)
  between operations  14.3 us (3%)
  other arithmetic  6.42 us (1%)
    ppermute x2, waiting for transfers between devices, passed_along(): return lax.ppermute(x, axis, pairs)  329 us
    reduce_scatter x1, waiting for transfers between devices, local(): lax.psum_scatter(partial_value, 'head', scatter_dimension=1, tiled=True)  66.1 us
    all_to_all x1, starting transfers between devices, local(): lax.all_to_all(jnp.stack([w_output for _ in range(lax.psum(1, 'ctx'))], a...  11.9 us
  transfers between devices with their start and end apart: 4, of which 2 were waited for; matrix products, arithmetic and copies ran while one was open for 6% of the time, Pallas kernels for 0%

profile of v1, /device:TPU:1, one launch (start us, length us, event | category | flops | bytes accessed | tf_op | source)
XLA Modules:
  0.0 486.6 jit_solution(13942027453409324577)
XLA Ops:
  6.5 0.0 copy-start
  6.5 8.3 %stack.2 = bf16[16,8,8,7168]{3,2,1,0:T(8,128)(2,1)} broadcast(bf16[8,8,7168]{2,1,0:T(8,128)(2,1)} %param.15), dimensions={1,2,3} | broadcast | bytes 15597568 | tf_op jit(solution)/shard_map/stack | solution.py:84
  14.9 0.0 copy-start.3
  14.9 0.0 slice-start
  14.9 0.0 copy-start.7
  14.9 11.9 %all-to-all-start = ((bf16[16,8,8,7168]{3,2,1,0:T(8,128)(2,1)}), bf16[16,8,8,7168]{3,2,1,0:T(8,128)(2,1)}, u32[]{:S(2)}, u32[]{:S(2)}) async-start(bf16[16,8,8,7168]{3,2,1,0:T(8,128)(2,1)} %stack.2), calls=%async_computation | async-start | bytes 29360128 | tf_op jit(solution)/shard_map/all_to_all | solution.py:83
  26.8 0.0 reduce-scatter.2.cloned.1.call-start
  26.9 0.0 copy-done.3
  26.9 0.2 multiply_cosine_fusion
  27.1 0.1 copy.43
  27.2 0.1 copy.42
  27.4 0.0 slice-done
  27.4 0.1 copy.59
  27.5 0.8 pad_maximum_fusion
  28.3 3.9 collective-permute-start.1
  32.3 4.0 collective-permute-start
  36.9 0.0 copy-done.7
  36.9 4.7 convolution_convert_fusion
  41.6 1.4 copy.45
  43.1 0.7 subtract_convert_fusion
  43.8 0.3 fusion.15
  44.1 1.1 constant_dynamic-slice_fusion.1
  45.2 0.2 copy.58
  45.4 0.2 copy.60
  45.6 329.3 %collective-permute-done = bf16[256,576]{1,0:T(8,128)(2,1)} collective-permute-done((bf16[256,576]{1,0:T(8,128)(2,1)}, bf16[256,576]{1,0:T(8,128)(2,1)}, u32[]{:S(2)}, u32[]{:S(2)}) %collective-permute-start) | collective-permute-done | bytes 294944 | tf_op jit(solution)/shard_map/ppermute | solution.py:10
  374.9 0.0 collective-permute-done.1
  374.9 0.1 broadcast_select_fusion
  375.0 0.0 copy-start.5
  375.0 1.1 maximum_maximum_fusion
  376.1 0.0 copy-done
  376.1 6.1 %fusion.2 = f32[768,256,8]{1,0,2:T(8,128)} fusion(bf16[8,128,512]{2,1,0:T(8,128)(2,1)S(1)} %copy-done, bf16[768,576]{1,0:T(8,128)(2,1)} %maximum_maximum_fusion, bf16[256,8,192]{0,2,1:T(8,128)(2,1)S(1)} %bitcast.32), kind=kOutput, calls=%fused_computation.6 | convolution fusion | flops 1880096768 | bytes 8650752 | tf_op jit(solution)/shard_map/thl,kl->htk/dot_general | solution.py:62
  382.2 0.0 copy-done.5
  382.2 4.0 bitcast_select_fusion
  386.2 0.0 copy-start.2
  386.3 2.6 copy-done.2
  388.9 0.0 copy-start.4
  388.9 0.0 copy-start.6
  388.9 1.1 fusion.32
  390.0 0.0 copy-done.4
  390.1 0.3 copy-done.6
  390.4 7.3 %fusion.9 = bf16[8,256,128]{1,2,0:T(8,128)(2,1)S(1)} fusion(bf16[8,512,128]{2,1,0:T(8,128)(2,1)S(1)} %copy-done.6, f32[8,256]{1,0:T(8,128)S(1)} %fusion.32, bf16[768,576]{1,0:T(8,128)(2,1)S(1)} %copy-done.4, f32[8,256,768]{1,2,0:T(8,128)} %copy-done.2), kind=kOutput, calls=%fused_computation.12 | convolution fusion | flops 1885080320 | bytes 14950400 | tf_op jit(solution)/shard_map/thl,hlv->thv/dot_general | solution.py:79
  397.7 0.0 all-to-all-done
  397.7 7.6 %copy.51 = bf16[16,8,8,7168]{3,2,0,1:T(8,128)(2,1)S(1)} copy(bf16[16,8,8,7168]{3,2,1,0:T(8,128)(2,1)} %all-to-all-done) | data formatting | bytes 29360128 | tf_op jit(solution)/shard_map/all_to_all | solution.py:83
  405.3 0.0 copy-start.1
  405.3 6.3 %fusion.33 = f32[256,7168]{1,0:T(8,128)} fusion(bf16[256,1024]{0,1:T(8,128)(2,1)S(1)} %bitcast.33, bf16[1024,7168]{1,0:T(8,128)(2,1)S(1)} %bitcast.30), kind=kOutput, calls=%fused_computation.53 | convolution fusion | flops 3758096384 | bytes 22544384 | tf_op jit(solution)/shard_map/dot_general | solution.py:90
  411.7 0.0 reduce-scatter.2.cloned.1.call-update
  411.7 66.1 %reduce-scatter.2.cloned.1.call-done = f32[256,896]{1,0:T(8,128)} async-done(((f32[256,7168]{1,0:T(8,128)}), f32[256,896]{1,0:T(8,128)}) %reduce-scatter.2.cloned.1.call-update) | async-done | bytes 917520 | tf_op jit(solution)/shard_map/reduce_scatter | solution.py:91
  477.8 2.0 convert_element_type.54
  479.8 0.0 copy-done.1
  (7 shorter events, 0.1 us)
Async XLA Ops:
  6.5 369.6 %copy-start = (bf16[8,128,512]{2,1,0:T(8,128)(2,1)S(1)}, bf16[8,128,512]{2,1,0:T(8,128)(2,1)}, u32[]{:S(2)}) copy-start(bf16[8,128,512]{2,1,0:T(8,128)(2,1)} %param.13) | copy-start | bytes 3145732
  14.9 12.0 %copy-start.3 = (bf16[256,576]{0,1:T(8,128)(2,1)S(1)}, bf16[256,576]{0,1:T(8,128)(2,1)}, u32[]{:S(2)}) copy-start(bf16[256,576]{0,1:T(8,128)(2,1)} %param.9) | copy-start | bytes 884740
  14.9 12.5 %slice-start = ((bf16[256,576]{0,1:T(8,128)(2,1)}), bf16[256,512]{0,1:T(8,128)(2,1)S(1)}, s32[]{:S(2)}) async-start(bf16[256,576]{0,1:T(8,128)(2,1)} %param.9), calls=%async_computation.3 | async-start | bytes 524288 | tf_op jit(solution)/shard_map/slice | solution.py:46
  14.9 22.1 %copy-start.7 = (bf16[256,1536]{1,0:T(8,128)(2,1)S(1)}, bf16[256,1536]{1,0:T(8,128)(2,1)}, u32[]{:S(2)}) copy-start(bf16[256,1536]{1,0:T(8,128)(2,1)} %param.8) | copy-start | bytes 2359300
  14.9 382.9 %all-to-all-start = ((bf16[16,8,8,7168]{3,2,1,0:T(8,128)(2,1)}), bf16[16,8,8,7168]{3,2,1,0:T(8,128)(2,1)}, u32[]{:S(2)}, u32[]{:S(2)}) async-start(bf16[16,8,8,7168]{3,2,1,0:T(8,128)(2,1)} %stack.2), calls=%async_computation | async-start | bytes 29360128 | tf_op jit(solution)/shard_map/all_to_all | solution.py:83
  26.8 451.0 %reduce-scatter.2.cloned.1.call-start = ((), (), s32[]{:S(2)}) async-start(), calls=%async_computation.2 | async-start | bytes 8257536 | tf_op jit(solution)/shard_map/reduce_scatter | solution.py:91
  28.3 346.6 %collective-permute-start.1 = (bf16[256,576]{1,0:T(8,128)(2,1)}, bf16[256,576]{1,0:T(8,128)(2,1)}, u32[]{:S(2)}, u32[]{:S(2)}) collective-permute-start(bf16[256,576]{1,0:T(8,128)(2,1)} %pad_maximum_fusion), channel_id=1, source_target_pairs={{0,16},{16,32},{32,48},{48,64},{64,80},{80,96},{96,112},{112,128},... | collective-permute-start | bytes 884744 | tf_op jit(solution)/shard_map/ppermute | solution.py:10
  32.3 342.6 %collective-permute-start = (bf16[256,576]{1,0:T(8,128)(2,1)}, bf16[256,576]{1,0:T(8,128)(2,1)}, u32[]{:S(2)}, u32[]{:S(2)}) collective-permute-start(bf16[256,576]{1,0:T(8,128)(2,1)} %pad_maximum_fusion), channel_id=1, source_target_pairs={{0,32},{16,48},{32,64},{48,80},{64,96},{80,112},{96,128},{112,144}... | collective-permute-start | bytes 884744 | tf_op jit(solution)/shard_map/ppermute | solution.py:10
  375.0 7.2 %copy-start.5 = (bf16[256,8,32]{0,2,1:T(8,128)(2,1)S(1)}, bf16[256,8,32]{0,2,1:T(8,128)(2,1)}, u32[]{:S(2)}) copy-start(bf16[256,8,32]{0,2,1:T(8,128)(2,1)} %get-tuple-element.6) | copy-start | bytes 393220
  386.2 2.6 copy-start.2
  388.9 1.2 copy-start.4
  388.9 1.5 copy-start.6
  405.3 74.4 %copy-start.1 = (bf16[8,128,512]{2,1,0:T(8,128)(2,1)S(1)}, bf16[8,128,512]{2,1,0:T(8,128)(2,1)}, u32[]{:S(2)}) copy-start(bf16[8,128,512]{2,1,0:T(8,128)(2,1)} %param.13) | copy-start | bytes 3145732
Sparse Core Ops, SparseCore 0:
  411.8 65.8 reduce-scatter.1
